TPU v7x, 256 devices: a whole 4x4x8 slice. The times are simulated.
256 devices in a mesh: row: 16 (over y, x_hi, core), col: 16 (over z, x_lo).
Axes of the slice: x: 4 (x_hi: 2, x_lo: 2; x = x_hi * 2 + x_lo), y: 4, z: 8, core: 2. Of those that a mesh axis runs over, the one named last changes fastest.
Arguments:
- pair_rep: bfloat16 [1024, 1024, 128], P('row', 'col'), may hold values from -6 to 6
- token_mask: int32 [1024], replicated, may hold values from 0 to 1, as said below
- in_gain: float32 [128], replicated, may hold values from 0.5 to 2
- in_bias: float32 [128], replicated, may hold values from -3 to 3
- left_weight: bfloat16 [128, 256], replicated, may hold values from -0.5 to 0.5
- right_weight: bfloat16 [128, 256], replicated, may hold values from -0.5 to 0.5
- gate_weight: bfloat16 [128, 128], replicated, may hold values from -0.5 to 0.5
- out_gain: float32 [128], replicated, may hold values from 0.5 to 2
- out_bias: float32 [128], replicated, may hold values from -3 to 3
- out_weight: bfloat16 [128, 128], replicated, may hold values from -0.5 to 0.5
Outputs:
- update: bfloat16 [1024, 1024, 128], P('row', 'col')
Inputs may be any that keep to these rules, and one draw needn't show every extreme that they name: `token_mask`: tokens lie in chains of 64 consecutive slots; in each chain a leading run of 32 to 64 slots is 1 and the rest is 0; the first chain is full and the second holds exactly 32 real tokens.
All inputs are finite; a program needn't handle non-finite values.
Results may differ from a plain program's by a relative error of at most 0.0053.
Values may be sent and summed in bfloat16 or wider, within the bound.
A program may use at most 128 MiB of HBM per device.

v0:
```python
import jax
import jax.numpy as jnp
from jax import lax
from jax.sharding import PartitionSpec as P

EPS = 1e-05


def layer_norm(values, gain_vec, bias_vec, along):
    average = jnp.mean(values, axis=along, keepdims=True)
    centered = values - average
    variance = jnp.mean(centered * centered, axis=along, keepdims=True)
    return centered * lax.rsqrt(variance + EPS) * gain_vec + bias_vec


def shards(
    pair_rep,
    token_mask,
    in_gain,
    in_bias,
    left_weight,
    right_weight,
    gate_weight,
    out_gain,
    out_bias,
    out_weight,
):
    row_tok, col_tok, pair_width = pair_rep.shape
    hidden_width = out_weight.shape[0]
    row_count = lax.axis_size("row")
    col_count = lax.axis_size("col")
    validity = token_mask.astype(jnp.float32)
    row_valid = lax.dynamic_slice_in_dim(validity, lax.axis_index("row") * row_tok, row_tok)
    col_valid = lax.dynamic_slice_in_dim(validity, lax.axis_index("col") * col_tok, col_tok)
    pair_mask = row_valid[:, None] * col_valid[None, :]
    normed = layer_norm(pair_rep.astype(jnp.float32), in_gain, in_bias, 2).astype(jnp.bfloat16)
    gate_value = jax.nn.sigmoid(
        jnp.einsum("ijc,cd->ijd", normed, gate_weight, preferred_element_type=jnp.float32)
    )
    left_proj = jnp.einsum("ijc,cg->ijg", normed, left_weight, preferred_element_type=jnp.float32)
    right_proj = jnp.einsum("ijc,cg->ijg", normed, right_weight, preferred_element_type=jnp.float32)
    left_value = (
        jax.nn.sigmoid(left_proj[..., :hidden_width])
        * left_proj[..., hidden_width:]
        * pair_mask[..., None]
    ).astype(jnp.bfloat16)
    right_value = (
        jax.nn.sigmoid(right_proj[..., :hidden_width])
        * right_proj[..., hidden_width:]
        * pair_mask[..., None]
    ).astype(jnp.bfloat16)
    slab_width = col_tok // row_count
    stacked = left_value.reshape(row_tok, row_count, 1, slab_width, hidden_width)
    left_panel = lax.all_gather(stacked, "col", axis=2, tiled=True)
    left_panel = left_panel.reshape(row_tok, row_count * col_count * slab_width, hidden_width)
    right_routed = lax.all_to_all(
        lax.all_to_all(right_value, "row", split_axis=1, concat_axis=0, tiled=True),
        "col",
        split_axis=0,
        concat_axis=1,
        tiled=True,
    )
    product = jnp.einsum(
        "ikh,jkh->ijh",
        left_panel,
        lax.all_gather(right_routed, "row", axis=1, tiled=True),
        preferred_element_type=jnp.float32,
    )
    final_norm = layer_norm(product, out_gain, out_bias, 2).astype(jnp.bfloat16)
    update = gate_value * jnp.einsum(
        "ijh,hc->ijc", final_norm, out_weight, preferred_element_type=jnp.float32
    )
    return update.astype(jnp.bfloat16)


def solution(mesh):
    placed = (P("row", "col", None), P(), P(), P(), P(), P(), P(), P(), P(), P())
    return jax.shard_map(
        shards, mesh=mesh, in_specs=placed, out_specs=P("row", "col", None), check_vma=False
    )
```

profile of v0, /device:TPU:1, one launch (start us, length us, event | category | flops | bytes accessed | tf_op | source)
XLA Modules:
  0.0 581.7 jit_solution(16728545810675229486)
XLA Ops:
  6.5 0.0 copy-start
  6.5 0.0 all-gather.5.cloned.1.call-start
  6.6 0.8 convert_element_type.23
  7.4 1.8 convert_reduce_fusion
  9.2 2.3 fusion.2
  11.6 0.0 copy-done
  11.6 0.0 copy-done.2
  11.6 0.0 copy-done.6
  11.6 0.0 copy-done.5
  11.6 0.0 copy-start.3
  11.6 3.3 fusion.16
  15.0 0.0 copy-done.3
  15.0 3.4 fusion.18
  18.3 0.1 fusion.26
  18.4 0.1 broadcast_multiply_fusion
  18.5 4.0 fusion.7
  22.5 1.7 copy.49
  24.2 0.0 all-gather.5.cloned.1.call-update
  24.2 0.0 all-gather.3.cloned.1.call-start
  24.3 0.7 copy.44
  25.0 44.1 %all_to_all.36 = bf16[64,64,128]{2,0,1:T(8,128)(2,1)S(1)} all-to-all(bf16[64,64,128]{2,0,1:T(8,128)(2,1)S(1)} %copy.44), channel_id=1, replica_groups=mesh['row'=16,'col'=16] {'row'}, dimensions={1} | all-to-all | bytes 2097152 | tf_op jit(solution)/shard_map/all_to_all | solution.py:57
  69.1 0.1 copy.45
  69.2 0.8 copy.46
  70.0 53.9 %all_to_all.37 = bf16[1024,4,128]{2,1,0:T(4,128)(2,1)S(1)} all-to-all(bf16[1024,4,128]{2,1,0:T(4,128)(2,1)S(1)} %copy.46), channel_id=1, replica_groups=mesh['row'=16,'col'=16] {'col'}, dimensions={0} | all-to-all | bytes 2097152 | tf_op jit(solution)/shard_map/all_to_all | solution.py:56
  123.9 0.1 copy.47
  124.0 0.0 copy-start.4
  124.0 1.1 copy.48
  125.1 0.0 all-gather.3.cloned.1.call-update
  125.1 0.0 copy-done.4
  125.1 2.5 fusion.21
  127.7 267.5 %all-gather.5.cloned.1.call-done = bf16[64,16,16,4,128]{4,0,3,2,1:T(8,128)(2,1)} async-done(((bf16[64,16,1,4,128]{4,0,3,2,1:T(8,128)(2,1)}), bf16[64,16,16,4,128]{4,0,3,2,1:T(8,128)(2,1)}) %all-gather.5.cloned.1.call-update) | async-done | bytes 16777232 | tf_op jit(solution)/shard_map/all_gather | solution.py:54
  395.2 26.0 %copy.51 = bf16[64,1024,128]{1,0,2:T(8,128)(2,1)} copy(bf16[64,1024,128]{2,0,1:T(8,128)(2,1)} %bitcast.32) | data formatting | bytes 33554432 | tf_op jit(solution)/shard_map/reshape | solution.py:55
  421.2 100.2 %all-gather.3.cloned.1.call-done = bf16[64,1024,128]{2,0,1:T(8,128)(2,1)} async-done(((bf16[64,64,128]{2,0,1:T(8,128)(2,1)}), bf16[64,1024,128]{2,0,1:T(8,128)(2,1)}) %all-gather.3.cloned.1.call-update) | async-done | bytes 16777232 | tf_op jit(solution)/shard_map/all_gather | solution.py:66
  521.3 26.0 %copy.50 = bf16[64,1024,128]{1,0,2:T(8,128)(2,1)} copy(bf16[64,1024,128]{2,0,1:T(8,128)(2,1)} %all-gather.3.cloned.1.call-done) | data formatting | bytes 33554432 | tf_op jit(solution)/shard_map/all_gather | solution.py:66
  547.3 14.9 %bitcast_reduce_fusion = (f32[64,64]{0,1:T(8,128)S(1)}, f32[128,64,64]{2,1,0:T(8,128)}) fusion(bf16[64,1024,128]{1,0,2:T(8,128)(2,1)} %copy.50, bf16[64,1024,128]{1,0,2:T(8,128)(2,1)} %copy.51), kind=kOutput, calls=%fused_computation.1 | convolution fusion | flops 1074262016 | bytes 35667968 | tf_op jit(solution)/shard_map/ikh,jkh->ijh/dot_general | solution.py:63
  562.3 0.1 copy.52
  562.3 0.1 copy.53
  562.4 0.0 copy-start.7
  562.4 0.0 copy-start.8
  562.4 2.8 multiply_reduce_fusion
  565.3 0.1 copy.54
  565.4 0.1 copy.55
  565.4 0.0 copy-done.7
  565.5 2.9 add_convert_fusion
  568.4 0.0 copy-start.9
  568.4 3.1 copy.56
  571.6 0.0 copy-start.1
  571.6 3.2 multiply_convert_fusion
  (10 shorter events, 0.1 us)
Async XLA Ops:
  6.5 5.1 copy-start
  6.5 5.1 copy-start.2
  6.5 5.1 copy-start.6
  6.5 5.1 copy-start.5
  6.5 388.7 %all-gather.5.cloned.1.call-start = ((), (), s32[]{:S(2)}) async-start(), calls=%async_computation.3 | async-start | bytes 17825792 | tf_op jit(solution)/shard_map/all_gather | solution.py:54
  11.6 3.4 copy-start.3
  24.2 497.1 %all-gather.3.cloned.1.call-start = ((), (), s32[]{:S(2)}) async-start(), calls=%async_computation.2 | async-start | bytes 17825792 | tf_op jit(solution)/shard_map/all_gather | solution.py:66
  124.0 1.1 copy-start.4
  562.4 3.0 copy-start.7
  562.4 3.0 copy-start.8
  568.4 3.2 copy-start.9
  571.6 3.3 copy-start.1
Sparse Core Ops, SparseCore 0:
  24.3 370.8 all-gather.4
  398.0 123.3 all-gather.2
where the time goes:
time: 583 us; the launch traced here: 582 us
  waiting for transfers between devices  368 us (63%)
  blocking collectives  98 us (17%)
  local copies, waits for them, and re-layouts  59.9 us (10%)
  matrix products  27.4 us (5%)
  other arithmetic  14.9 us (3%)
  between operations  13.6 us (2%)
    all_gather x1, waiting for transfers between devices, shards(): left_panel = lax.all_gather(stacked, 'col', axis=2, tiled=True)  268 us
    all_gather x1, waiting for transfers between devices, shards(): lax.all_gather(right_routed, 'row', axis=1, tiled=True)  100 us
    all_to_all x1, blocking collectives, shards(): lax.all_to_all(lax.all_to_all(right_value, 'row', split_axis=1, concat_ax...  53.9 us
    all_to_all x1, blocking collectives, shards(): lax.all_to_all(right_value, 'row', split_axis=1, concat_axis=0, tiled=True)  44.1 us
    all_gather x1, local copies, waits for them, and re-layouts, shards(): lax.all_gather(right_routed, 'row', axis=1, tiled=True)  26 us
    reshape x1, local copies, waits for them, and re-layouts, shards(): left_panel.reshape(row_tok, row_count * col_count * slab_width, hidden_wi...  26 us
    dot_general x1, matrix products, shards(): jnp.einsum('ikh,jkh->ijh', left_panel, lax.all_gather(right_routed, 'row'...  14.9 us
  transfers between devices with their start and end apart: 2, of which 2 were waited for; matrix products, arithmetic and copies ran while one was open for 5% of the time, Pallas kernels for 0%

commit v1 on v0

v1 whole, which is shorter than its diff:
```python
import functools

import jax
import jax.numpy as jnp
from jax import lax
from jax.experimental import pallas as pl
from jax.experimental.pallas import tpu as pltpu
from jax.sharding import PartitionSpec as P

EPS = 1e-05
MESH = pl.DeviceIdType.MESH
F32 = jnp.float32
BF16 = jnp.bfloat16
NT = (((1,), (1,)), ((), ()))
TN = (((0,), (0,)), ((), ()))

ROWS = 16
COLS = 16
CHIPS = 8
DEPTHS = 8
TOK = 64
WIDTH = 128
HALF = 8


def sigmoid(v):
    return 0.5 * jnp.tanh(0.5 * v) + 0.5


def shift_of(step):
    away = (step + 1) // 2
    return lax.rem(4 + (1 - 2 * lax.rem(step, 2)) * away, DEPTHS)


def exchange_kernel(
    x_ref, w_ref, wg_ref, ln_ref, m_ref,
    q_ref, gate_ref,
    t_buf, s_buf, x_buf, acc, p_buf, gate_buf,
    gate_sem, s_send, s_recv, f_send, f_recv, p_send, p_recv,
):
    row, col = lax.axis_index("row"), lax.axis_index("col")
    core, half, chip, slot = lax.rem(row, 2), row // HALF, row // 2, lax.rem(row, HALF)
    depth, side = col // 2, lax.rem(col, 2)
    me = row * COLS + col
    sibling = row + 1 - 2 * core
    channel = chip * COLS + col

    barrier = pltpu.get_barrier_semaphore()

    def greet(t, carry):
        other = lax.rem(me + t, ROWS * COLS)
        pl.semaphore_signal(
            barrier, inc=1, device_id=(other // COLS, lax.rem(other, COLS)), device_id_type=MESH
        )
        return carry

    lax.fori_loop(1, ROWS * COLS, greet, 0)

    gain, bias = ln_ref[0:1, :], ln_ref[1:2, :]
    blank = jnp.zeros((TOK, WIDTH), BF16)

    def project(q, carry):
        v = x_ref[pl.ds(2 * q, 2)].reshape(2 * TOK, WIDTH).astype(F32)
        v = v - jnp.mean(v, axis=-1, keepdims=True)
        spread = jnp.mean(v * v, axis=-1, keepdims=True)
        n = (v * lax.rsqrt(spread + EPS) * gain + bias).astype(BF16)
        gate = sigmoid(jnp.dot(n, wg_ref[...], preferred_element_type=F32))
        gate_buf[pl.ds(2 * q, 2)] = gate.reshape(2, TOK, WIDTH)
        a, b = n[:TOK], n[TOK:]
        both = jnp.concatenate(
            [jnp.concatenate([a, blank, b, blank], 0), jnp.concatenate([blank, a, blank, b], 0)], 1
        )
        d = lax.dot_general(w_ref[...], both, NT, preferred_element_type=F32)
        e = sigmoid(d[:WIDTH]) * d[WIDTH:]
        base = pl.multiple_of(q * 2 * WIDTH, 2 * WIDTH)
        t_buf[pl.ds(base, WIDTH), :] = e[:, :WIDTH] * m_ref[pl.ds(2 * q, 1), :]
        t_buf[pl.ds(base + WIDTH, WIDTH), :] = e[:, WIDTH:] * m_ref[pl.ds(2 * q + 1, 1), :]
        return carry

    lax.fori_loop(0, TOK // 2, project, 0)
    gate_copy = pltpu.make_async_copy(gate_buf, gate_ref, gate_sem)
    gate_copy.start()

    def by_channel(h, carry):
        s_buf[h] = t_buf[pl.ds(h, TOK, stride=WIDTH), :].astype(BF16)
        return carry

    lax.fori_loop(0, WIDTH, by_channel, 0)

    pl.semaphore_wait(barrier, ROWS * COLS - 1)

    def send(step, t):
        to_chip = lax.rem(chip + t // 2, CHIPS)
        to_col = lax.rem(depth + shift_of(step), DEPTHS) * 2 + lax.rem(side + t, 2)
        to_row = to_chip * 2 + half
        src, dst = s_buf.at[to_chip * COLS + to_col], x_buf.at[col, row]
        mine = jnp.logical_and(to_row == row, to_col == col)

        @pl.when(mine)
        def _():
            pltpu.make_async_copy(src, dst, s_recv.at[step]).start()

        @pl.when(jnp.logical_not(mine))
        def _():
            pltpu.make_async_remote_copy(
                src_ref=src, dst_ref=dst, send_sem=s_send, recv_sem=s_recv.at[step],
                device_id=(to_row, to_col), device_id_type=MESH,
            ).start()

    def send_one(step, t, carry):
        send(step, t)
        return carry

    def send_two(u, carry):
        step = 1 + 2 * (u // 16)
        send(step, lax.rem(u, 16))
        send(step + 1, lax.rem(u, 16))
        return carry

    lax.fori_loop(0, 16, functools.partial(send_one, 0), 0)
    lax.fori_loop(0, 48, send_two, 0)
    lax.fori_loop(0, 16, functools.partial(send_one, 7), 0)

    lanes = lax.broadcasted_iota(jnp.int32, (HALF * TOK, WIDTH), 1)

    def first_col(step):
        return lax.rem(depth - shift_of(step) + DEPTHS, DEPTHS) * 2

    def forward(step):
        part = x_buf.at[pl.ds(first_col(step), 2), pl.ds(core * HALF, HALF)]
        return pltpu.make_async_remote_copy(
            src_ref=part, dst_ref=part, send_sem=f_send.at[step], recv_sem=f_recv.at[step],
            device_id=(sibling, col), device_id_type=MESH,
        )

    def arrive(step):
        part = x_buf.at[pl.ds(first_col(step), 2), pl.ds(core * HALF, HALF)]
        pltpu.make_async_copy(part, part, s_recv.at[step]).wait()
        forward(step).start()

    def multiply(step, first):
        forward(step).wait_recv()
        c = first_col(step)
        wide = []
        for e in range(2):
            own = x_buf[c + e, pl.ds(core * HALF, HALF)].reshape(HALF * TOK, WIDTH).astype(F32)
            wide.append(jnp.where(lanes >= TOK, pltpu.roll(own, TOK, 1), 0.0).astype(BF16))
        own = jnp.concatenate(wide, 1)

        def block(n, carry):
            others = jnp.concatenate(
                [x_buf[c + e, pl.ds(4 * n, 4)].reshape(4 * TOK, WIDTH) for e in range(2)], 1
            )
            part = lax.dot_general(own, others, NT, preferred_element_type=F32)
            acc[n] = part if first else acc[n] + part
            return carry

        lax.fori_loop(0, 4, block, 0)

    arrive(0)
    arrive(1)
    multiply(0, True)

    def middle(step, carry):
        arrive(step + 1)
        multiply(step, False)
        return carry

    lax.fori_loop(1, DEPTHS - 1, middle, 0)
    multiply(DEPTHS - 1, False)

    low = lanes[: TOK // 2] < TOK

    def give(u, carry):
        r = lax.rem(slot + u, HALF)
        for n in range(4):
            for m in range(2):
                v = acc[n, pl.ds(pl.multiple_of(r * TOK, TOK), TOK), m * WIDTH : (m + 1) * WIDTH]
                top, bot = v[: TOK // 2], v[TOK // 2 :]
                even = jnp.where(low, top, pltpu.roll(bot, TOK, 1))
                odd = jnp.where(low, pltpu.roll(top, TOK, 1), bot)
                p_buf[r, 4 * n + 2 * m] = even.astype(BF16)
                p_buf[r, 4 * n + 2 * m + 1] = odd.astype(BF16)

        to_row = core * HALF + r

        def give_one(t, carry):
            step = t // 2
            to_col = lax.rem(depth + shift_of(step), DEPTHS) * 2 + lax.rem(side + t, 2)
            src, dst = p_buf.at[r, to_col], q_ref.at[channel]
            mine = jnp.logical_and(to_row == row, to_col == col)

            @pl.when(mine)
            def _():
                pltpu.make_async_copy(src, dst, p_recv).start()

            @pl.when(jnp.logical_not(mine))
            def _():
                pltpu.make_async_remote_copy(
                    src_ref=src, dst_ref=dst, send_sem=p_send, recv_sem=p_recv,
                    device_id=(to_row, to_col), device_id_type=MESH,
                ).start()

            return carry

        lax.fori_loop(0, COLS, give_one, 0)
        return carry

    lax.fori_loop(0, HALF, give, 0)

    gate_copy.wait()
    pltpu.make_async_copy(q_ref, q_ref, p_recv).wait()

    def drain(step, carry):
        forward(step).wait_send()
        return carry

    lax.fori_loop(0, DEPTHS, drain, 0)
    count = WIDTH - 1
    itself = half == core

    @pl.when(itself)
    def _():
        sent = s_buf.at[pl.ds(0, count)]
        pltpu.make_async_copy(sent, sent, s_send).wait()
        given = q_ref.at[pl.ds(0, count)]
        pltpu.make_async_copy(given, given, p_send).wait()

    @pl.when(jnp.logical_not(itself))
    def _():
        pltpu.make_async_copy(s_buf, s_buf, s_send).wait()
        pltpu.make_async_copy(q_ref, q_ref, p_send).wait()


def exchange(pair, w, wg, ln, mask):
    whole = pl.BlockSpec(memory_space=pltpu.VMEM)
    return pl.pallas_call(
        exchange_kernel,
        out_shape=(
            jax.ShapeDtypeStruct((WIDTH, TOK // 2, WIDTH), BF16),
            jax.ShapeDtypeStruct((TOK, TOK, WIDTH), F32),
        ),
        in_specs=[whole] * 5,
        out_specs=(pl.BlockSpec(memory_space=pl.ANY), pl.BlockSpec(memory_space=pl.ANY)),
        scratch_shapes=[
            pltpu.VMEM((TOK * WIDTH, WIDTH), F32),
            pltpu.VMEM((WIDTH, TOK, WIDTH), BF16),
            pltpu.VMEM((COLS, ROWS, TOK, WIDTH), BF16),
            pltpu.VMEM((4, HALF * TOK, 4 * TOK), F32),
            pltpu.VMEM((HALF, COLS, TOK // 2, WIDTH), BF16),
            pltpu.VMEM((TOK, TOK, WIDTH), F32),
            pltpu.SemaphoreType.DMA,
            pltpu.SemaphoreType.DMA,
            pltpu.SemaphoreType.DMA((DEPTHS,)),
            pltpu.SemaphoreType.DMA((DEPTHS,)),
            pltpu.SemaphoreType.DMA((DEPTHS,)),
            pltpu.SemaphoreType.DMA,
            pltpu.SemaphoreType.DMA,
        ],
        compiler_params=pltpu.CompilerParams(collective_id=0, has_side_effects=True),
        name="exchange",
    )(pair, w, wg, ln, mask)


CHUNK = 8


def update_kernel(q_ref, gate_ref, g_ref, b_ref, w_ref, out_ref, buf):
    v = q_ref[...].astype(F32)
    v = v - jnp.mean(v, axis=0, keepdims=True)
    spread = jnp.mean(v * v, axis=0, keepdims=True)
    n = v * lax.rsqrt(spread + EPS) * g_ref[...] + b_ref[...]
    buf[...] = n.reshape(WIDTH * CHUNK, WIDTH)
    for q in range(CHUNK):
        n = buf[pl.ds(q, WIDTH, stride=CHUNK), :].astype(BF16)
        o = lax.dot_general(n, w_ref[...], TN, preferred_element_type=F32)
        out_ref[0, q] = (gate_ref[0, q] * o[:TOK]).astype(BF16)
        out_ref[1, q] = (gate_ref[1, q] * o[TOK:]).astype(BF16)


def finish(q, gate, gain, bias, w):
    whole = lambda shape: pl.BlockSpec(shape, lambda i: (0,) * len(shape))
    part = pl.BlockSpec((2, CHUNK, TOK, WIDTH), lambda i: (0, i, 0, 0))
    return pl.pallas_call(
        update_kernel,
        out_shape=jax.ShapeDtypeStruct((2, TOK // 2, TOK, WIDTH), BF16),
        grid=(TOK // 2 // CHUNK,),
        in_specs=[
            pl.BlockSpec((WIDTH, CHUNK, WIDTH), lambda i: (0, i, 0)),
            part,
            whole((WIDTH, 1, WIDTH)),
            whole((WIDTH, 1, WIDTH)),
            whole((WIDTH, WIDTH)),
        ],
        out_specs=part,
        scratch_shapes=[pltpu.VMEM((WIDTH * CHUNK, WIDTH), F32)],
        name="finish",
    )(q, gate, gain, bias, w)


def shards(
    pair_rep,
    token_mask,
    in_gain,
    in_bias,
    left_weight,
    right_weight,
    gate_weight,
    out_gain,
    out_bias,
    out_weight,
):
    valid = token_mask.astype(F32)
    row_valid = lax.dynamic_slice_in_dim(valid, lax.axis_index("row") * TOK, TOK)
    col_valid = lax.dynamic_slice_in_dim(valid, lax.axis_index("col") * TOK, TOK)
    mask = row_valid[:, None] * jnp.tile(col_valid, 2)[None, :]
    w = jnp.concatenate([left_weight.T, right_weight.T], axis=1)
    ln = jnp.stack([in_gain, in_bias])
    q, gate = exchange(pair_rep, w, gate_weight, ln, mask)
    spread = lambda v: jnp.broadcast_to(v[:, None, None], (WIDTH, 1, WIDTH))
    out = finish(
        q, gate.reshape(2, TOK // 2, TOK, WIDTH), spread(out_gain), spread(out_bias), out_weight
    )
    return out.reshape(TOK, TOK, WIDTH)


def solution(mesh):
    placed = (P("row", "col", None), P(), P(), P(), P(), P(), P(), P(), P(), P())
    return jax.shard_map(
        shards, mesh=mesh, in_specs=placed, out_specs=P("row", "col", None), check_vma=False
    )
```

time: 583 us -> 128 us (0.22)
  waiting for transfers between devices: 368 us -> 0 us
  Pallas kernels: 0 us -> 120 us
  blocking collectives: 98 us -> 0 us
  local copies, waits for them, and re-layouts: 59.9 us -> 5.01 us
  matrix products: 27.4 us -> 0 us
  between operations: 13.6 us -> 0.03 us
  other arithmetic: 14.9 us -> 3.3 us
    all_gather x2 -> x0, waiting for transfers between devices: 368 us -> none  [the longest x1 268 us: shards(): left_panel = lax.all_gather(stacked, 'col', axis=2, tiled=True)]
    pallas_call x0 -> x2, Pallas kernels: none -> 120 us  [the longest x1 115 us: exchange(): pl.pallas_call(exchange_kernel, out_shape=(jax.ShapeDtypeStruct((WIDTH, T...]
    all_to_all x2 -> x0, blocking collectives: 98 us -> none  [the longest x1 53.9 us: shards(): lax.all_to_all(lax.all_to_all(right_value, 'row', split_axis=1, concat_ax...]
    reshape x2 -> x0, local copies, waits for them, and re-layouts: 27.6 us -> none  [the longest x1 26 us: shards(): left_panel.reshape(row_tok, row_count * col_count * slab_width, hidden_wi...]
    dot_general x5 -> x0, matrix products: 27.4 us -> none  [the longest x1 14.9 us: shards(): jnp.einsum('ikh,jkh->ijh', left_panel, lax.all_gather(right_routed, 'row'...]
    all_gather x1 -> x0, local copies, waits for them, and re-layouts: 26 us -> none  [shards(): lax.all_gather(right_routed, 'row', axis=1, tiled=True)]
    convert_element_type x3 -> x1, other arithmetic: 7.75 us -> 0.69 us  [shards(): valid = token_mask.astype(F32)]
    reduce_sum x3 -> x0, other arithmetic: 6.99 us -> none  [the longest x2 5.15 us: layer_norm(): variance = jnp.mean(centered * centered, axis=along, keepdims=True)]
  transfers between devices with their start and end apart: 2 -> 0, of which waited for: 2 -> 0; matrix products, arithmetic and copies ran while one was open for 5% -> 0% of each run, Pallas kernels for 0% -> 0%
where the time goes in v1:
time: 128 us
  Pallas kernels  120 us (94%)
  local copies, waits for them, and re-layouts  5.01 us (4%)
  other arithmetic  3.3 us (3%)
    pallas_call x1, Pallas kernels, exchange(): pl.pallas_call(exchange_kernel, out_shape=(jax.ShapeDtypeStruct((WIDTH, T...  115 us
    pallas_call x1, Pallas kernels, finish(): pl.pallas_call(update_kernel, out_shape=jax.ShapeDtypeStruct((2, TOK // 2...  5.09 us
    broadcast_in_dim x2, local copies, waits for them, and re-layouts, shards(): spread = lambda v: jnp.broadcast_to(v[:, None, None], (WIDTH, 1, WIDTH))  2.94 us

profile of v1, /device:TPU:1, one launch (start us, length us, event | category | flops | bytes accessed | tf_op | source)
XLA Modules:
  0.0 128.0 jit_solution(12177315440829568447)
XLA Ops:
  0.0 1.3 pad_maximum_fusion.1.ln_ref
  1.3 0.7 convert_element_type.3
  1.9 0.1 fusion
  2.0 0.1 mul.24
  2.1 0.7 broadcast_multiply_fusion.m_ref
  2.8 0.9 copy.11
  3.7 1.0 copy.12
  4.7 0.7 pad_maximum_fusion.w_ref
  5.4 1.5 %broadcast_in_dim.4.g_ref = f32[128,1,128]{2,1,0:T(1,128)} broadcast(f32[128]{0:T(128)} %param.17), dimensions={0} | broadcast | bytes 66048 | tf_op jit(solution)/shard_map/broadcast_in_dim | solution.py:320
  6.9 1.5 %broadcast_in_dim.5.b_ref = f32[128,1,128]{2,1,0:T(1,128)} broadcast(f32[128]{0:T(128)} %param.18), dimensions={0} | broadcast | bytes 66048 | tf_op jit(solution)/shard_map/broadcast_in_dim | solution.py:320
  8.3 114.5 %exchange.1 = (bf16[128,32,128]{2,1,0:T(8,128)(2,1)}, f32[64,64,128]{2,1,0:T(8,128)}) custom-call(bf16[64,64,128]{2,1,0:T(8,128)(2,1)} %x_ref.1, bf16[256,256]{1,0:T(8,128)(2,1)} %pad_maximum_fusion.w_ref, bf16[128,128]{1,0:T(8,128)(2,1)} %wg_ref.1, f32[2,128]{1,0:T(2,128)} %pad_maximum_fusion.1.ln_ref, f32[64,128]{1,0:T(8,128)} %broadcast_multiply_fusion.m_ref), custom_call_target="tpu_custom_call" | custom-call | tf_op jit(solution)/shard_map/exchange/pallas_call | solution.py:237
  122.9 5.1 %finish.1 = bf16[2,32,64,128]{3,2,1,0:T(8,128)(2,1)} custom-call(bf16[128,32,128]{2,1,0:T(8,128)(2,1)} %get-tuple-element.7.q_ref, f32[2,32,64,128]{3,2,1,0:T(8,128)} %bitcast.6, f32[128,1,128]{2,1,0:T(1,128)} %broadcast_in_dim.4.g_ref, f32[128,1,128]{2,1,0:T(1,128)} %broadcast_in_dim.5.b_ref, bf16[128,128]{1,0:T(8,128)(2,1)} %w_ref.1), custom_call_target="tpu_custom_call" | custom-call | tf_op jit(solution)/shard_map/finish/pallas_call | solution.py:284
  (1 shorter events, 0.0 us)

commit v2 on v1

v2 whole, which is shorter than its diff:
```python
import functools

import jax
import jax.numpy as jnp
from jax import lax
from jax.experimental import pallas as pl
from jax.experimental.pallas import tpu as pltpu
from jax.sharding import PartitionSpec as P

EPS = 1e-05
MESH = pl.DeviceIdType.MESH
F32 = jnp.float32
BF16 = jnp.bfloat16
NT = (((1,), (1,)), ((), ()))
TN = (((0,), (0,)), ((), ()))

ROWS = 16
COLS = 16
CHIPS = 8
DEPTHS = 8
TOK = 64
WIDTH = 128
HALF = 8


def sigmoid(v):
    return 0.5 * jnp.tanh(0.5 * v) + 0.5


SHIFTS = (4, 3, 5, 2, 6, 1, 7, 0)
PARTS = 4
PART = TOK // PARTS


def shift_of(step):
    away = (step + 1) // 2
    return lax.rem(4 + (1 - 2 * lax.rem(step, 2)) * away, DEPTHS)


def exchange_kernel(
    mask_ref, x_ref, wl_ref, wr_ref, wg_ref, gain_ref, bias_ref, valid_ref,
    q_ref, gate_ref,
    n_buf, t_buf, s_buf, x_buf, acc, p_buf, gate_buf,
    gate_sem, s_send, s_recv, f_send, f_recv, p_send, p_recv,
):
    row, col = lax.axis_index("row"), lax.axis_index("col")
    core, half, chip, slot = lax.rem(row, 2), row // HALF, row // 2, lax.rem(row, HALF)
    depth, side = col // 2, lax.rem(col, 2)
    sibling = row + 1 - 2 * core
    channel = chip * COLS + col
    itself = half == core
    apart = jnp.logical_not(itself)

    barrier = pltpu.get_barrier_semaphore()

    def hello(to_row, to_col):
        pl.semaphore_signal(barrier, inc=1, device_id=(to_row, to_col), device_id_type=MESH)

    def greet(c, carry):
        for r in range(HALF):
            to_row = core * HALF + r
            pl.when(jnp.logical_not(jnp.logical_and(to_row == row, c == col)))(
                functools.partial(hello, to_row, c)
            )
        return carry

    lax.fori_loop(0, COLS, greet, 0)
    pl.when(apart)(functools.partial(hello, sibling, col))

    gain, bias = gain_ref[...], bias_ref[...]
    wide = 2 * WIDTH
    eye = lax.broadcasted_iota(jnp.int32, (wide, wide), 0)
    eye = jnp.where(eye == lax.broadcasted_iota(jnp.int32, (wide, wide), 1), 1.0, 0.0).astype(BF16)
    weight = jnp.concatenate(
        [
            lax.dot_general(eye, w[...], NT, preferred_element_type=F32).astype(BF16)
            for w in (wl_ref, wr_ref)
        ],
        1,
    )
    blank = jnp.zeros((TOK, WIDTH), BF16)
    lane = lax.broadcasted_iota(jnp.int32, (1, WIDTH), 1)
    held = valid_ref[pl.ds(depth, 1), :].astype(F32)
    near = jnp.where(side == 0, 1, 0) == jnp.where(lane < TOK, 1, 0)
    held = jnp.where(near, held, pltpu.roll(held, TOK, 1))

    def project(part):
        for u in range(PART // 2):
            i = part * PART + 2 * u
            v = x_ref[pl.ds(i, 2)].reshape(2 * TOK, WIDTH).astype(F32)
            v = v - jnp.mean(v, axis=-1, keepdims=True)
            spread = jnp.mean(v * v, axis=-1, keepdims=True)
            n = (v * lax.rsqrt(spread + EPS) * gain + bias).astype(BF16)
            n_buf[pl.ds(i, 2)] = n.reshape(2, TOK, WIDTH)
            a, b = n[:TOK], n[TOK:]
            both = jnp.concatenate(
                [
                    jnp.concatenate([a, blank, b, blank], 0),
                    jnp.concatenate([blank, a, blank, b], 0),
                ],
                1,
            )
            d = lax.dot_general(weight, both, NT, preferred_element_type=F32)
            e = sigmoid(d[:WIDTH]) * d[WIDTH:]
            for k in range(2):
                m = held * mask_ref[row * TOK + i + k].astype(F32)
                t_buf[2 * u + k] = (e[:, k * WIDTH : (k + 1) * WIDTH] * m).astype(BF16)
        s_buf[:, pl.ds(part * PART, PART), :] = jnp.swapaxes(t_buf[...], 0, 1)

    chips = [lax.rem(chip + d, CHIPS) for d in range(CHIPS)]
    sides = [side, 1 - side]

    def send_to(part, step, d, to_col, alone):
        rows = pl.ds(part * PART, PART)
        src = s_buf.at[chips[d] * COLS + to_col, rows]
        dst = x_buf.at[col, row, rows]

        def remote():
            pltpu.make_async_remote_copy(
                src_ref=src, dst_ref=dst, send_sem=s_send, recv_sem=s_recv.at[step],
                device_id=(chips[d] * 2 + half, to_col), device_id_type=MESH,
            ).start()

        def local():
            pltpu.make_async_copy(src, dst, s_recv.at[step]).start()

        if alone:
            pl.when(itself)(local)
            pl.when(apart)(remote)
        else:
            remote()

    def send(part):
        far = lax.rem(depth + 4, DEPTHS) * 2
        for d in range(CHIPS):
            for e in range(2):
                send_to(part, 0, d, far + sides[e], False)

        def pair(u, carry):
            down = lax.rem(depth + 4 - u, DEPTHS) * 2
            up = lax.rem(depth + 4 + u, DEPTHS) * 2
            for d in range(CHIPS):
                for e in range(2):
                    send_to(part, 2 * u - 1, d, down + sides[e], False)
                    send_to(part, 2 * u, d, up + sides[e], False)
            return carry

        lax.fori_loop(1, 4, pair, 0)
        for d in range(CHIPS):
            for e in range(2):
                send_to(part, 7, d, depth * 2 + sides[e], d == 0 and e == 0)

    project(0)
    pl.semaphore_wait(barrier, CHIPS * COLS)
    send(0)

    def rest(part, carry):
        project(part)
        send(part)
        return carry

    lax.fori_loop(1, PARTS, rest, 0)

    def gates(u, carry):
        n = n_buf[pl.ds(4 * u, 4)].reshape(4 * TOK, WIDTH)
        gate = sigmoid(jnp.dot(n, wg_ref[...], preferred_element_type=F32))
        gate_buf[pl.ds(4 * u, 4)] = gate.reshape(4, TOK, WIDTH)
        return carry

    lax.fori_loop(0, TOK // 4, gates, 0)
    gate_copy = pltpu.make_async_copy(gate_buf, gate_ref, gate_sem)
    gate_copy.start()

    lanes = lax.broadcasted_iota(jnp.int32, (HALF * TOK, WIDTH), 1)

    def first_col(step):
        return lax.rem(depth - shift_of(step) + DEPTHS, DEPTHS) * 2

    def forward(step):
        part = x_buf.at[pl.ds(first_col(step), 2), pl.ds(core * HALF, HALF)]
        return pltpu.make_async_remote_copy(
            src_ref=part, dst_ref=part, send_sem=f_send.at[step], recv_sem=f_recv.at[step],
            device_id=(sibling, col), device_id_type=MESH,
        )

    def arrive(step):
        part = x_buf.at[pl.ds(first_col(step), 2), pl.ds(core * HALF, HALF)]
        pltpu.make_async_copy(part, part, s_recv.at[step]).wait()
        forward(step).start()

    def multiply(step, first):
        forward(step).wait_recv()
        c = first_col(step)
        own = []
        for e in range(2):
            v = x_buf[c + e, pl.ds(core * HALF, HALF)].reshape(HALF * TOK, WIDTH).astype(F32)
            own.append(jnp.where(lanes >= TOK, pltpu.roll(v, TOK, 1), 0.0).astype(BF16))
        own = jnp.concatenate(own, 1)

        def block(n, carry):
            others = jnp.concatenate(
                [x_buf[c + e, pl.ds(4 * n, 4)].reshape(4 * TOK, WIDTH) for e in range(2)], 1
            )
            part = lax.dot_general(own, others, NT, preferred_element_type=F32)
            acc[n] = part if first else acc[n] + part
            return carry

        lax.fori_loop(0, 4, block, 0)

    arrive(0)
    arrive(1)
    multiply(0, True)

    def middle(step, carry):
        arrive(step + 1)
        multiply(step, False)
        return carry

    lax.fori_loop(1, DEPTHS - 1, middle, 0)
    multiply(DEPTHS - 1, False)

    low = lanes[: TOK // 2] < TOK
    targets = [
        lax.rem(depth + shift, DEPTHS) * 2 + sides[e] for shift in SHIFTS for e in range(2)
    ]

    def give(u, carry):
        r = lax.rem(slot + u, HALF)
        for n in range(4):
            for m in range(2):
                v = acc[n, pl.ds(pl.multiple_of(r * TOK, TOK), TOK), m * WIDTH : (m + 1) * WIDTH]
                top, bot = v[: TOK // 2], v[TOK // 2 :]
                even = jnp.where(low, top, pltpu.roll(bot, TOK, 1))
                odd = jnp.where(low, pltpu.roll(top, TOK, 1), bot)
                p_buf[r, 4 * n + 2 * m] = even.astype(BF16)
                p_buf[r, 4 * n + 2 * m + 1] = odd.astype(BF16)
        to_row = core * HALF + r
        for k, to_col in enumerate(targets):
            src, dst = p_buf.at[r, to_col], q_ref.at[channel]

            def remote(src=src, dst=dst, to_col=to_col):
                pltpu.make_async_remote_copy(
                    src_ref=src, dst_ref=dst, send_sem=p_send, recv_sem=p_recv,
                    device_id=(to_row, to_col), device_id_type=MESH,
                ).start()

            def local(src=src, dst=dst):
                pltpu.make_async_copy(src, dst, p_recv).start()

            if SHIFTS[k // 2] == 0 and k % 2 == 0:
                here = to_row == row
                pl.when(here)(local)
                pl.when(jnp.logical_not(here))(remote)
            else:
                remote()
        return carry

    lax.fori_loop(0, HALF, give, 0)

    gate_copy.wait()
    pltpu.make_async_copy(q_ref, q_ref, p_recv).wait()

    def drain(step, carry):
        forward(step).wait_send()
        return carry

    lax.fori_loop(0, DEPTHS, drain, 0)

    @pl.when(itself)
    def _():
        sent = s_buf.at[pl.ds(0, WIDTH - 1)]
        pltpu.make_async_copy(sent, sent, s_send).wait()
        given = q_ref.at[pl.ds(0, WIDTH - 1)]
        pltpu.make_async_copy(given, given, p_send).wait()

    @pl.when(apart)
    def _():
        pltpu.make_async_copy(s_buf, s_buf, s_send).wait()
        pltpu.make_async_copy(q_ref, q_ref, p_send).wait()


def exchange(mask, pair, wl, wr, wg, gain, bias):
    whole = pl.BlockSpec(memory_space=pltpu.VMEM)
    return pl.pallas_call(
        exchange_kernel,
        out_shape=(
            jax.ShapeDtypeStruct((WIDTH, TOK // 2, WIDTH), BF16),
            jax.ShapeDtypeStruct((TOK, TOK, WIDTH), F32),
        ),
        in_specs=[pl.BlockSpec(memory_space=pltpu.SMEM)] + [whole] * 7,
        out_specs=(pl.BlockSpec(memory_space=pl.ANY), pl.BlockSpec(memory_space=pl.ANY)),
        scratch_shapes=[
            pltpu.VMEM((TOK, TOK, WIDTH), BF16),
            pltpu.VMEM((PART, WIDTH, WIDTH), BF16),
            pltpu.VMEM((WIDTH, TOK, WIDTH), BF16),
            pltpu.VMEM((COLS, ROWS, TOK, WIDTH), BF16),
            pltpu.VMEM((4, HALF * TOK, 4 * TOK), F32),
            pltpu.VMEM((HALF, COLS, TOK // 2, WIDTH), BF16),
            pltpu.VMEM((TOK, TOK, WIDTH), F32),
            pltpu.SemaphoreType.DMA,
            pltpu.SemaphoreType.DMA,
            pltpu.SemaphoreType.DMA((DEPTHS,)),
            pltpu.SemaphoreType.DMA((DEPTHS,)),
            pltpu.SemaphoreType.DMA((DEPTHS,)),
            pltpu.SemaphoreType.DMA,
            pltpu.SemaphoreType.DMA,
        ],
        compiler_params=pltpu.CompilerParams(collective_id=0, has_side_effects=True),
        name="exchange",
    )(mask, pair, wl, wr, wg, gain, bias, mask.reshape(DEPTHS, WIDTH))


CHUNK = 8


def update_kernel(q_ref, gate_ref, g_ref, b_ref, w_ref, out_ref, wide):
    @pl.when(pl.program_id(0) == 0)
    def _():
        wide[0] = jnp.broadcast_to(g_ref[...], (WIDTH, WIDTH)).T
        wide[1] = jnp.broadcast_to(b_ref[...], (WIDTH, WIDTH)).T

    turned = jnp.swapaxes(q_ref[...], 0, 1)
    for q in range(CHUNK):
        v = turned[q].astype(F32)
        v = v - jnp.mean(v, axis=0, keepdims=True)
        spread = jnp.mean(v * v, axis=0, keepdims=True)
        n = (v * lax.rsqrt(spread + EPS) * wide[0] + wide[1]).astype(BF16)
        o = lax.dot_general(n, w_ref[...], TN, preferred_element_type=F32)
        out_ref[0, q] = (gate_ref[0, q] * o[:TOK]).astype(BF16)
        out_ref[1, q] = (gate_ref[1, q] * o[TOK:]).astype(BF16)


def finish(q, gate, gain, bias, w):
    whole = lambda shape: pl.BlockSpec(shape, lambda i: (0,) * len(shape))
    part = pl.BlockSpec((2, CHUNK, TOK, WIDTH), lambda i: (0, i, 0, 0))
    return pl.pallas_call(
        update_kernel,
        out_shape=jax.ShapeDtypeStruct((2, TOK // 2, TOK, WIDTH), BF16),
        grid=(TOK // 2 // CHUNK,),
        in_specs=[
            pl.BlockSpec((WIDTH, CHUNK, WIDTH), lambda i: (0, i, 0)),
            part,
            whole((1, WIDTH)),
            whole((1, WIDTH)),
            whole((WIDTH, WIDTH)),
        ],
        out_specs=part,
        scratch_shapes=[pltpu.VMEM((2, WIDTH, WIDTH), F32)],
        name="finish",
    )(q, gate, gain, bias, w)


def shards(
    pair_rep,
    token_mask,
    in_gain,
    in_bias,
    left_weight,
    right_weight,
    gate_weight,
    out_gain,
    out_bias,
    out_weight,
):
    flat = lambda v: v.reshape(1, WIDTH)
    q, gate = exchange(
        token_mask, pair_rep, left_weight, right_weight, gate_weight, flat(in_gain), flat(in_bias)
    )
    out = finish(
        q, gate.reshape(2, TOK // 2, TOK, WIDTH), flat(out_gain), flat(out_bias), out_weight
    )
    return out.reshape(TOK, TOK, WIDTH)


def solution(mesh):
    placed = (P("row", "col", None), P(), P(), P(), P(), P(), P(), P(), P(), P())
    return jax.shard_map(
        shards, mesh=mesh, in_specs=placed, out_specs=P("row", "col", None), check_vma=False
    )
```

time: 128 us -> 104 us (0.81)
  Pallas kernels: 120 us -> 104 us
  local copies, waits for them, and re-layouts: 5.01 us -> 0 us
  other arithmetic: 3.3 us -> 0 us
    pallas_call x1, Pallas kernels: 115 us -> 99 us  [exchange(): pl.pallas_call(exchange_kernel, out_shape=(jax.ShapeDtypeStruct((WIDTH, T...]
    broadcast_in_dim x2 -> x0, local copies, waits for them, and re-layouts: 2.94 us -> none  [shards(): spread = lambda v: jnp.broadcast_to(v[:, None, None], (WIDTH, 1, WIDTH))]
    unnamed x2 -> x0, local copies, waits for them, and re-layouts: 1.9 us -> none
where the time goes in v2:
time: 104 us
  Pallas kernels  104 us (100%)
    pallas_call x1, Pallas kernels, exchange(): pl.pallas_call(exchange_kernel, out_shape=(jax.ShapeDtypeStruct((WIDTH, T...  99 us
    pallas_call x1, Pallas kernels, finish(): pl.pallas_call(update_kernel, out_shape=jax.ShapeDtypeStruct((2, TOK // 2...  4.69 us

profile of v2, /device:TPU:1, one launch (start us, length us, event | category | flops | bytes accessed | tf_op | source)
XLA Modules:
  0.0 103.7 jit_solution(8652813598540925296)
XLA Ops:
  0.0 99.0 %exchange.1 = (bf16[128,32,128]{2,1,0:T(8,128)(2,1)}, f32[64,64,128]{2,1,0:T(8,128)}) custom-call(s32[1024]{0:T(1024)} %mask_ref.1, bf16[64,64,128]{2,1,0:T(8,128)(2,1)} %x_ref.1, bf16[128,256]{1,0:T(8,128)(2,1)} %wl_ref.1, bf16[128,256]{1,0:T(8,128)(2,1)} %wr_ref.1, bf16[128,128]{1,0:T(8,128)(2,1)} %wg_ref.1, f32[1,128]{1,0:T(1,128)} %bitcast.9, ...), custom_call_target="tpu_custom_call" | custom-call | tf_op jit(solution)/shard_map/exchange/pallas_call | solution.py:284
  99.0 4.7 %finish.1 = bf16[2,32,64,128]{3,2,1,0:T(8,128)(2,1)} custom-call(bf16[128,32,128]{2,1,0:T(8,128)(2,1)} %get-tuple-element.7.q_ref, f32[2,32,64,128]{3,2,1,0:T(8,128)} %bitcast.7, f32[1,128]{1,0:T(1,128)} %bitcast.11, f32[1,128]{1,0:T(1,128)} %bitcast.12, bf16[128,128]{1,0:T(8,128)(2,1)} %w_ref.1), custom_call_target="tpu_custom_call" | custom-call | tf_op jit(solution)/shard_map/finish/pallas_call | solution.py:336

commit v3 on v2

v3 whole, which is shorter than its diff:
```python
import functools

import jax
import jax.numpy as jnp
from jax import lax
from jax.experimental import pallas as pl
from jax.experimental.pallas import tpu as pltpu
from jax.sharding import PartitionSpec as P

EPS = 1e-05
MESH = pl.DeviceIdType.MESH
F32 = jnp.float32
BF16 = jnp.bfloat16
NT = (((1,), (1,)), ((), ()))
TN = (((0,), (0,)), ((), ()))

ROWS = 16
COLS = 16
CHIPS = 8
DEPTHS = 8
TOK = 64
WIDTH = 128
HALF = 8


def sigmoid(v):
    return 0.5 * jnp.tanh(0.5 * v) + 0.5


SHIFTS = (4, 3, 5, 2, 6, 1, 7, 0)
PARTS = 2
LINES = TOK // 2
PART = LINES // PARTS


def shift_of(step):
    away = (step + 1) // 2
    return lax.rem(4 + (1 - 2 * lax.rem(step, 2)) * away, DEPTHS)


def exchange_kernel(
    mask_ref, x_ref, wl_ref, wr_ref, wg_ref, gain_ref, bias_ref, valid_ref,
    q_ref, gate_ref,
    n_buf, tr_buf, tl_buf, sr_buf, sl_buf, xr_buf, xl_buf, r_buf, p_buf, gate_buf,
    gate_sem, r_send, l_send, r_recv, l_recv, f_send, f_recv, p_send, p_recv,
):
    row, col = lax.axis_index("row"), lax.axis_index("col")
    core, half, chip, slot = lax.rem(row, 2), row // HALF, row // 2, lax.rem(row, HALF)
    depth, side = col // 2, lax.rem(col, 2)
    sibling = row + 1 - 2 * core
    channel = chip * COLS + col
    itself = half == core
    apart = jnp.logical_not(itself)

    barrier = pltpu.get_barrier_semaphore()

    def hello(to_row, to_col):
        pl.semaphore_signal(barrier, inc=1, device_id=(to_row, to_col), device_id_type=MESH)

    def greet(c, carry):
        for r in range(HALF):
            to_row = core * HALF + r
            pl.when(jnp.logical_not(jnp.logical_and(to_row == row, c == col)))(
                functools.partial(hello, to_row, c)
            )
        return carry

    lax.fori_loop(0, COLS, greet, 0)
    pl.when(apart)(functools.partial(hello, sibling, col))

    gain, bias = gain_ref[...], bias_ref[...]
    wide = 2 * WIDTH
    eye = lax.broadcasted_iota(jnp.int32, (wide, wide), 0)
    eye = jnp.where(eye == lax.broadcasted_iota(jnp.int32, (wide, wide), 1), 1.0, 0.0).astype(BF16)
    weight = jnp.concatenate(
        [
            lax.dot_general(eye, w[...], NT, preferred_element_type=F32).astype(BF16)
            for w in (wl_ref, wr_ref)
        ],
        1,
    )
    blank = jnp.zeros((TOK, WIDTH), BF16)
    lane = lax.broadcasted_iota(jnp.int32, (1, WIDTH), 1)
    held = valid_ref[pl.ds(depth, 1), :].astype(F32)
    near = jnp.where(side == 0, 1, 0) == jnp.where(lane < TOK, 1, 0)
    held = jnp.where(near, held, pltpu.roll(held, TOK, 1))

    left_half = lane < TOK

    def project(part):
        def eight(w, carry):
            for u in range(8):
                line = part * PART + 8 * w + u
                first, second = line + LINES * side, line + LINES * (1 - side)
                v = jnp.concatenate([x_ref[first], x_ref[second]], 0).astype(F32)
                v = v - jnp.mean(v, axis=-1, keepdims=True)
                spread = jnp.mean(v * v, axis=-1, keepdims=True)
                n = (v * lax.rsqrt(spread + EPS) * gain + bias).astype(BF16)
                n_buf[first] = n[:TOK]
                n_buf[second] = n[TOK:]
                empty = jnp.concatenate([blank, blank], 0)
                both = jnp.concatenate(
                    [jnp.concatenate([empty, n], 0), jnp.concatenate([n, empty], 0)], 1
                )
                d = lax.dot_general(weight, both, NT, preferred_element_type=F32)
                e = sigmoid(d[:WIDTH]) * d[WIDTH:]
                one = mask_ref[row * TOK + first].astype(F32)
                two = mask_ref[row * TOK + second].astype(F32)
                m = held * jnp.where(left_half, one, two)
                tr_buf[8 * w + u] = (e[:, :WIDTH] * m).astype(BF16)
                tl_buf[8 * w + u] = (e[:, WIDTH:] * m).astype(BF16)
            return carry

        lax.fori_loop(0, PART // 8, eight, 0)
        rows = pl.ds(part * PART, PART)
        sr_buf[:, rows, :] = jnp.swapaxes(tr_buf[...], 0, 1)
        sl_buf[:, rows, :] = jnp.swapaxes(tl_buf[...], 0, 1)

    chips = [lax.rem(chip + d, CHIPS) for d in range(CHIPS)]
    sides = [side, 1 - side]

    def send(buf, dst, send_sem, sem_of, part):
        rows = pl.ds(part * PART, PART)

        def send_to(step, d, to_col, alone):
            src = buf.at[chips[d] * COLS + to_col, rows]

            def remote():
                pltpu.make_async_remote_copy(
                    src_ref=src, dst_ref=dst, send_sem=send_sem, recv_sem=sem_of(step),
                    device_id=(chips[d] * 2 + half, to_col), device_id_type=MESH,
                ).start()

            def local():
                pltpu.make_async_copy(src, dst, sem_of(step)).start()

            if alone:
                pl.when(itself)(local)
                pl.when(apart)(remote)
            else:
                remote()

        far = lax.rem(depth + 4, DEPTHS) * 2
        for d in range(CHIPS):
            for e in range(2):
                send_to(0, d, far + sides[e], False)

        def pair(u, carry):
            down = lax.rem(depth + 4 - u, DEPTHS) * 2
            up = lax.rem(depth + 4 + u, DEPTHS) * 2
            for d in range(CHIPS):
                for e in range(2):
                    send_to(2 * u - 1, d, down + sides[e], False)
                    send_to(2 * u, d, up + sides[e], False)
            return carry

        lax.fori_loop(1, 4, pair, 0)
        for d in range(CHIPS):
            for e in range(2):
                send_to(7, d, depth * 2 + sides[e], d == 0 and e == 0)

    def send_right(part):
        dst = xr_buf.at[col, row, pl.ds(part * PART, PART)]
        send(sr_buf, dst, r_send, lambda step: r_recv.at[step], part)

    def send_left(part, carry):
        dst = xl_buf.at[col, slot, pl.ds(part * PART, PART)]
        send(sl_buf, dst, l_send, lambda step: l_recv.at[part], part)
        return carry

    project(0)
    pl.semaphore_wait(barrier, CHIPS * COLS)
    send_right(0)
    project(1)
    send_right(1)
    lax.fori_loop(0, PARTS, send_left, 0)

    def gates(u, carry):
        n = n_buf[pl.ds(4 * u, 4)].reshape(4 * TOK, WIDTH)
        gate = sigmoid(jnp.dot(n, wg_ref[...], preferred_element_type=F32))
        gate_buf[pl.ds(4 * u, 4)] = gate.reshape(4, TOK, WIDTH)
        return carry

    lax.fori_loop(0, TOK // 4, gates, 0)
    gate_copy = pltpu.make_async_copy(gate_buf, gate_ref, gate_sem)
    gate_copy.start()

    def forward(step):
        c = lax.rem(depth - shift_of(step) + DEPTHS, DEPTHS) * 2
        part = xr_buf.at[pl.ds(c, 2), pl.ds(core * HALF, HALF)]
        return part, pltpu.make_async_remote_copy(
            src_ref=part, dst_ref=part, send_sem=f_send.at[step], recv_sem=f_recv.at[step],
            device_id=(sibling, col), device_id_type=MESH,
        )

    def arrive(step, carry):
        part, copy = forward(step)
        pltpu.make_async_copy(part, part, r_recv.at[step]).wait()
        copy.start()
        return carry

    lax.fori_loop(0, DEPTHS, arrive, 0)

    def arrive_too(step, carry):
        forward(step)[1].wait_recv()
        return carry

    lax.fori_loop(0, DEPTHS, arrive_too, 0)

    def straight(even, odd, lanes):
        even, odd = even.astype(F32), odd.astype(F32)
        top = jnp.where(lanes, even, odd).astype(BF16)
        bot = pltpu.roll(jnp.where(lanes, odd, even), TOK, 1).astype(BF16)
        return top, bot

    def align_right(z, carry):
        for k in range(4):
            even, odd = (
                xr_buf[2 * z + e, 4 * k : 4 * k + 4].reshape(4 * LINES, WIDTH) for e in range(2)
            )
            top, bot = straight(even, odd, left_half)
            both = [v.reshape(4, LINES, WIDTH) for v in (top, bot)]
            r_buf[z, 4 * TOK * k : 4 * TOK * (k + 1), :] = jnp.concatenate(both, 1).reshape(
                4 * TOK, WIDTH
            )
        return carry

    lax.fori_loop(0, DEPTHS, align_right, 0)

    targets = [
        lax.rem(depth + shift, DEPTHS) * 2 + sides[e] for shift in SHIFTS for e in range(2)
    ]

    def multiply(part):
        rows = pl.ds(part * PART, PART)
        arrived = xl_buf.at[:, :, rows]
        pltpu.make_async_copy(arrived, arrived, l_recv.at[part]).wait()
        own = []
        for z in range(DEPTHS):
            even, odd = (
                xl_buf[2 * z + e, :, rows, :].reshape(HALF * PART, WIDTH) for e in range(2)
            )
            both = [v.reshape(HALF, PART, WIDTH) for v in straight(even, odd, left_half)]
            own.append(jnp.concatenate(both, 1).reshape(HALF * 2 * PART, WIDTH))
        own = jnp.concatenate(own, 1)

        def block(n, carry):
            start = pl.multiple_of(n * 4 * TOK, 4 * TOK)
            others = jnp.concatenate([r_buf[z, pl.ds(start, 4 * TOK), :] for z in range(DEPTHS)], 1)
            v = lax.dot_general(own, others, NT, preferred_element_type=F32)
            for r in range(HALF):
                for m in range(2):
                    w = v[2 * PART * r : 2 * PART * (r + 1), m * WIDTH : (m + 1) * WIDTH]
                    top, bot = w[:PART], w[PART:]
                    even = jnp.where(left_half, top, pltpu.roll(bot, TOK, 1))
                    odd = jnp.where(left_half, pltpu.roll(top, TOK, 1), bot)
                    p_buf[part, r, 4 * n + 2 * m] = even.astype(BF16)
                    p_buf[part, r, 4 * n + 2 * m + 1] = odd.astype(BF16)
            return carry

        lax.fori_loop(0, 4, block, 0)

    def give(part):
        def one_row(u, carry):
            r = lax.rem(slot + u, HALF)
            to_row = core * HALF + r
            dst = q_ref.at[channel, pl.ds(part * PART, PART)]
            for k, to_col in enumerate(targets):
                src = p_buf.at[part, r, to_col]

                def remote(src=src, to_col=to_col):
                    pltpu.make_async_remote_copy(
                        src_ref=src, dst_ref=dst,
                        send_sem=p_send.at[part], recv_sem=p_recv.at[part],
                        device_id=(to_row, to_col), device_id_type=MESH,
                    ).start()

                def local(src=src):
                    pltpu.make_async_copy(src, dst, p_recv.at[part]).start()

                if SHIFTS[k // 2] == 0 and k % 2 == 0:
                    here = to_row == row
                    pl.when(here)(local)
                    pl.when(jnp.logical_not(here))(remote)
                else:
                    remote()
            return carry

        lax.fori_loop(0, HALF, one_row, 0)

    def product(part, carry):
        multiply(part)
        give(part)
        return carry

    lax.fori_loop(0, PARTS, product, 0)

    gate_copy.wait()

    def drain(step, carry):
        forward(step)[1].wait_send()
        return carry

    lax.fori_loop(0, DEPTHS, drain, 0)

    def finished(n):
        for buf, sem in ((sr_buf, r_send), (sl_buf, l_send)):
            sent = buf.at[pl.ds(0, n)]
            pltpu.make_async_copy(sent, sent, sem).wait()
        for part in range(PARTS):
            given = q_ref.at[pl.ds(0, n), pl.ds(part * PART, PART)]
            pltpu.make_async_copy(given, given, p_send.at[part]).wait()

    pl.when(itself)(functools.partial(finished, WIDTH - 1))
    pl.when(apart)(functools.partial(finished, WIDTH))
    for part in range(PARTS):
        come = q_ref.at[:, pl.ds(part * PART, PART)]
        pltpu.make_async_copy(come, come, p_recv.at[part]).wait()


def exchange(mask, pair, wl, wr, wg, gain, bias):
    whole = pl.BlockSpec(memory_space=pltpu.VMEM)
    return pl.pallas_call(
        exchange_kernel,
        out_shape=(
            jax.ShapeDtypeStruct((WIDTH, TOK // 2, WIDTH), BF16),
            jax.ShapeDtypeStruct((TOK, TOK, WIDTH), F32),
        ),
        in_specs=[pl.BlockSpec(memory_space=pltpu.SMEM)] + [whole] * 7,
        out_specs=(pl.BlockSpec(memory_space=pl.ANY), pl.BlockSpec(memory_space=pl.ANY)),
        scratch_shapes=[
            pltpu.VMEM((TOK, TOK, WIDTH), BF16),
            pltpu.VMEM((PART, WIDTH, WIDTH), BF16),
            pltpu.VMEM((PART, WIDTH, WIDTH), BF16),
            pltpu.VMEM((WIDTH, LINES, WIDTH), BF16),
            pltpu.VMEM((WIDTH, LINES, WIDTH), BF16),
            pltpu.VMEM((COLS, ROWS, LINES, WIDTH), BF16),
            pltpu.VMEM((COLS, HALF, LINES, WIDTH), BF16),
            pltpu.VMEM((DEPTHS, ROWS * TOK, WIDTH), BF16),
            pltpu.VMEM((PARTS, HALF, COLS, PART, WIDTH), BF16),
            pltpu.VMEM((TOK, TOK, WIDTH), F32),
            pltpu.SemaphoreType.DMA,
            pltpu.SemaphoreType.DMA,
            pltpu.SemaphoreType.DMA,
            pltpu.SemaphoreType.DMA((DEPTHS,)),
            pltpu.SemaphoreType.DMA((PARTS,)),
            pltpu.SemaphoreType.DMA((DEPTHS,)),
            pltpu.SemaphoreType.DMA((DEPTHS,)),
            pltpu.SemaphoreType.DMA((PARTS,)),
            pltpu.SemaphoreType.DMA((PARTS,)),
        ],
        compiler_params=pltpu.CompilerParams(collective_id=0, has_side_effects=True),
        name="exchange",
    )(mask, pair, wl, wr, wg, gain, bias, mask.reshape(DEPTHS, WIDTH))


CHUNK = 8


def update_kernel(q_ref, gate_ref, g_ref, b_ref, w_ref, out_ref, wide):
    @pl.when(pl.program_id(0) == 0)
    def _():
        wide[0] = jnp.broadcast_to(g_ref[...], (WIDTH, WIDTH)).T
        wide[1] = jnp.broadcast_to(b_ref[...], (WIDTH, WIDTH)).T

    turned = jnp.swapaxes(q_ref[...], 0, 1)
    for q in range(CHUNK):
        v = turned[q].astype(F32)
        v = v - jnp.mean(v, axis=0, keepdims=True)
        spread = jnp.mean(v * v, axis=0, keepdims=True)
        n = (v * lax.rsqrt(spread + EPS) * wide[0] + wide[1]).astype(BF16)
        o = lax.dot_general(n, w_ref[...], TN, preferred_element_type=F32)
        out_ref[0, q] = (gate_ref[0, q] * o[:TOK]).astype(BF16)
        out_ref[1, q] = (gate_ref[1, q] * o[TOK:]).astype(BF16)


def finish(q, gate, gain, bias, w):
    whole = lambda shape: pl.BlockSpec(shape, lambda i: (0,) * len(shape))
    part = pl.BlockSpec((2, CHUNK, TOK, WIDTH), lambda i: (0, i, 0, 0))
    return pl.pallas_call(
        update_kernel,
        out_shape=jax.ShapeDtypeStruct((2, TOK // 2, TOK, WIDTH), BF16),
        grid=(TOK // 2 // CHUNK,),
        in_specs=[
            pl.BlockSpec((WIDTH, CHUNK, WIDTH), lambda i: (0, i, 0)),
            part,
            whole((1, WIDTH)),
            whole((1, WIDTH)),
            whole((WIDTH, WIDTH)),
        ],
        out_specs=part,
        scratch_shapes=[pltpu.VMEM((2, WIDTH, WIDTH), F32)],
        name="finish",
    )(q, gate, gain, bias, w)


def shards(
    pair_rep,
    token_mask,
    in_gain,
    in_bias,
    left_weight,
    right_weight,
    gate_weight,
    out_gain,
    out_bias,
    out_weight,
):
    flat = lambda v: v.reshape(1, WIDTH)
    q, gate = exchange(
        token_mask, pair_rep, left_weight, right_weight, gate_weight, flat(in_gain), flat(in_bias)
    )
    out = finish(
        q, gate.reshape(2, TOK // 2, TOK, WIDTH), flat(out_gain), flat(out_bias), out_weight
    )
    return out.reshape(TOK, TOK, WIDTH)


def solution(mesh):
    placed = (P("row", "col", None), P(), P(), P(), P(), P(), P(), P(), P(), P())
    return jax.shard_map(
        shards, mesh=mesh, in_specs=placed, out_specs=P("row", "col", None), check_vma=False
    )
```

time: 104 us -> 91.3 us (0.88)
  Pallas kernels: 104 us -> 91.1 us
    pallas_call x1, Pallas kernels: 99 us -> 86.4 us  [exchange(): pl.pallas_call(exchange_kernel, out_shape=(jax.ShapeDtypeStruct((WIDTH, T...]
where the time goes in v3:
time: 91.3 us; the launch traced here: 91.1 us
  Pallas kernels  91.1 us (100%)
    pallas_call x1, Pallas kernels, exchange(): pl.pallas_call(exchange_kernel, out_shape=(jax.ShapeDtypeStruct((WIDTH, T...  86.4 us
    pallas_call x1, Pallas kernels, finish(): pl.pallas_call(update_kernel, out_shape=jax.ShapeDtypeStruct((2, TOK // 2...  4.69 us

profile of v3, /device:TPU:1, one launch (start us, length us, event | category | flops | bytes accessed | tf_op | source)
XLA Modules:
  0.0 91.1 jit_solution(13692212364307796656)
XLA Ops:
  0.0 86.4 %exchange.1 = (bf16[128,32,128]{2,1,0:T(8,128)(2,1)}, f32[64,64,128]{2,1,0:T(8,128)}) custom-call(s32[1024]{0:T(1024)} %mask_ref.1, bf16[64,64,128]{2,1,0:T(8,128)(2,1)} %x_ref.1, bf16[128,256]{1,0:T(8,128)(2,1)} %wl_ref.1, bf16[128,256]{1,0:T(8,128)(2,1)} %wr_ref.1, bf16[128,128]{1,0:T(8,128)(2,1)} %wg_ref.1, f32[1,128]{1,0:T(1,128)} %bitcast.9, ...), custom_call_target="tpu_custom_call" | custom-call | tf_op jit(solution)/shard_map/exchange/pallas_call | solution.py:323
  86.4 4.7 %finish.1 = bf16[2,32,64,128]{3,2,1,0:T(8,128)(2,1)} custom-call(bf16[128,32,128]{2,1,0:T(8,128)(2,1)} %get-tuple-element.7.q_ref, f32[2,32,64,128]{3,2,1,0:T(8,128)} %bitcast.7, f32[1,128]{1,0:T(1,128)} %bitcast.11, f32[1,128]{1,0:T(1,128)} %bitcast.12, bf16[128,128]{1,0:T(8,128)(2,1)} %w_ref.1), custom_call_target="tpu_custom_call" | custom-call | tf_op jit(solution)/shard_map/finish/pallas_call | solution.py:380

commit v4 on v3

v4 whole, which is shorter than its diff:
```python
import functools

import jax
import jax.numpy as jnp
from jax import lax
from jax.experimental import pallas as pl
from jax.experimental.pallas import tpu as pltpu
from jax.sharding import PartitionSpec as P

EPS = 1e-05
MESH = pl.DeviceIdType.MESH
F32 = jnp.float32
BF16 = jnp.bfloat16
NT = (((1,), (1,)), ((), ()))
TN = (((0,), (0,)), ((), ()))

ROWS = 16
COLS = 16
CHIPS = 8
DEPTHS = 8
TOK = 64
WIDTH = 128
LIMIT = 60 * 1024 * 1024
HALF = 8


def sigmoid(v):
    return 0.5 * jnp.tanh(0.5 * v) + 0.5


REACH = 4
PARTS = 2
LINES = TOK // 2
PART = LINES // PARTS


def exchange_kernel(
    mask_ref, x_ref, wl_ref, wr_ref, wg_ref, gain_ref, bias_ref, valid_ref,
    og_ref, ob_ref, ow_ref,
    out_ref,
    n_buf, tr_buf, tl_buf, sr_buf, sl_buf, xr_buf, xl_buf, r_buf, p_buf, q_ref, gate_buf, wide_buf, out_buf,
    kept, given_buf, taken,
    out_sem, r_send, l_send, r_recv, l_recv, f_send, f_recv, p_send, p_recv,
    e_send, e_recv,
):
    row, col = lax.axis_index("row"), lax.axis_index("col")
    core, half, chip, slot = lax.rem(row, 2), row // HALF, row // 2, lax.rem(row, HALF)
    depth, side = col // 2, lax.rem(col, 2)
    sibling = row + 1 - 2 * core
    above = lax.rem(depth + 1, DEPTHS) * 2 + side
    below = lax.rem(depth + DEPTHS - 1, DEPTHS) * 2 + side
    channels = (chip * COLS + col, chip * COLS + below)
    itself = half == core
    apart = jnp.logical_not(itself)

    barrier = pltpu.get_barrier_semaphore()

    def hello(to_row, to_col):
        pl.semaphore_signal(barrier, inc=1, device_id=(to_row, to_col), device_id_type=MESH)

    def greet(t, carry):
        to_col = lax.rem(col + t, COLS)
        for r in range(HALF):
            hello(core * HALF + r, to_col)
        return carry

    lax.fori_loop(1, COLS, greet, 0)
    for r in range(HALF):
        pl.when(core * HALF + r != row)(functools.partial(hello, core * HALF + r, col))

    @pl.when(apart)
    def _():
        hello(sibling, col)
        hello(row, above)
        hello(row, below)


    gain, bias = gain_ref[...], bias_ref[...]
    wide = 2 * WIDTH
    eye = lax.broadcasted_iota(jnp.int32, (wide, wide), 0)
    eye = jnp.where(eye == lax.broadcasted_iota(jnp.int32, (wide, wide), 1), 1.0, 0.0).astype(BF16)
    weight = jnp.concatenate(
        [
            lax.dot_general(eye, w[...], NT, preferred_element_type=F32).astype(BF16)
            for w in (wl_ref, wr_ref)
        ],
        1,
    )
    blank = jnp.zeros((TOK, WIDTH), BF16)
    lane = lax.broadcasted_iota(jnp.int32, (1, WIDTH), 1)
    held = valid_ref[pl.ds(depth, 1), :].astype(F32)
    near = jnp.where(side == 0, 1, 0) == jnp.where(lane < TOK, 1, 0)
    held = jnp.where(near, held, pltpu.roll(held, TOK, 1))

    left_half = lane < TOK

    def project(part):
        def eight(w, carry):
            for u in range(8):
                line = part * PART + 8 * w + u
                first, second = line + LINES * side, line + LINES * (1 - side)
                v = jnp.concatenate([x_ref[first], x_ref[second]], 0).astype(F32)
                v = v - jnp.mean(v, axis=-1, keepdims=True)
                spread = jnp.mean(v * v, axis=-1, keepdims=True)
                n = (v * lax.rsqrt(spread + EPS) * gain + bias).astype(BF16)
                n_buf[first] = n[:TOK]
                n_buf[second] = n[TOK:]
                empty = jnp.concatenate([blank, blank], 0)
                both = jnp.concatenate(
                    [jnp.concatenate([empty, n], 0), jnp.concatenate([n, empty], 0)], 1
                )
                d = lax.dot_general(weight, both, NT, preferred_element_type=F32)
                e = sigmoid(d[:WIDTH]) * d[WIDTH:]
                one = mask_ref[row * TOK + first].astype(F32)
                two = mask_ref[row * TOK + second].astype(F32)
                m = held * jnp.where(left_half, one, two)
                tr_buf[8 * w + u] = (e[:, :WIDTH] * m).astype(BF16)
                tl_buf[8 * w + u] = (e[:, WIDTH:] * m).astype(BF16)
            return carry

        lax.fori_loop(0, PART // 8, eight, 0)
        rows = pl.ds(part * PART, PART)
        sr_buf[:, rows, :] = jnp.swapaxes(tr_buf[...], 0, 1)
        sl_buf[:, rows, :] = jnp.swapaxes(tl_buf[...], 0, 1)

    chips = [lax.rem(chip + d, CHIPS) for d in range(CHIPS)]
    sides = [side, 1 - side]

    def send(buf, dst_of, send_sem, sem_of, part):
        rows = pl.ds(part * PART, PART)

        def send_to(role, reach, d, e, alone):
            plane = lax.rem(depth + (reach if role == 0 else DEPTHS - reach), DEPTHS)
            owner = plane if role == 0 else lax.rem(plane + DEPTHS - 1, DEPTHS)
            src = buf.at[chips[d] * COLS + owner * 2 + sides[e], rows]
            step = role * REACH + reach
            dst = dst_of(step)

            def remote():
                pltpu.make_async_remote_copy(
                    src_ref=src, dst_ref=dst, send_sem=send_sem, recv_sem=sem_of(step),
                    device_id=(chips[d] * 2 + half, plane * 2 + sides[e]), device_id_type=MESH,
                ).start()

            def local():
                pltpu.make_async_copy(src, dst, sem_of(step)).start()

            if alone:
                pl.when(itself)(local)
                pl.when(apart)(remote)
            else:
                remote()

        def far(u, carry):
            for d in range(CHIPS):
                for e in range(2):
                    for role in range(2):
                        send_to(role, REACH - 1 - u, d, e, False)
            return carry

        lax.fori_loop(0, REACH - 1, far, 0)
        for d in range(CHIPS):
            for e in range(2):
                for role in range(2):
                    send_to(role, 0, d, e, d == 0 and e == 0)

    def send_right(part):
        rows = pl.ds(part * PART, PART)
        send(
            sr_buf, lambda step: xr_buf.at[step, side, row, rows],
            r_send, lambda step: r_recv.at[step], part,
        )

    def send_left(part, carry):
        rows = pl.ds(part * PART, PART)
        send(
            sl_buf, lambda step: xl_buf.at[step, side, slot, rows],
            l_send, lambda step: l_recv.at[part], part,
        )
        return carry

    project(0)

    @pl.when(itself)
    def _():
        pl.semaphore_wait(barrier, CHIPS * COLS)

    @pl.when(apart)
    def _():
        pl.semaphore_wait(barrier, CHIPS * COLS + 2)

    send_right(0)
    project(1)
    send_right(1)
    lax.fori_loop(0, PARTS, send_left, 0)

    def gates(u, carry):
        n = n_buf[pl.ds(4 * u, 4)].reshape(4 * TOK, WIDTH)
        gate = sigmoid(jnp.dot(n, wg_ref[...], preferred_element_type=F32))
        gate_buf[pl.ds(4 * u, 4)] = gate.reshape(4, TOK, WIDTH)
        return carry

    lax.fori_loop(0, TOK // 4, gates, 0)
    wide_buf[0] = jnp.broadcast_to(og_ref[...], (WIDTH, WIDTH)).T
    wide_buf[1] = jnp.broadcast_to(ob_ref[...], (WIDTH, WIDTH)).T

    def forward(step):
        part = xr_buf.at[step, :, pl.ds(core * HALF, HALF)]
        return part, pltpu.make_async_remote_copy(
            src_ref=part, dst_ref=part, send_sem=f_send.at[step], recv_sem=f_recv.at[step],
            device_id=(sibling, col), device_id_type=MESH,
        )

    def arrive(step, carry):
        part, copy = forward(step)
        pltpu.make_async_copy(part, part, r_recv.at[step]).wait()
        copy.start()
        return carry

    lax.fori_loop(0, DEPTHS, arrive, 0)

    def arrive_too(step, carry):
        forward(step)[1].wait_recv()
        return carry

    lax.fori_loop(0, DEPTHS, arrive_too, 0)

    def straight(even, odd, lanes):
        even, odd = even.astype(F32), odd.astype(F32)
        top = jnp.where(lanes, even, odd).astype(BF16)
        bot = pltpu.roll(jnp.where(lanes, odd, even), TOK, 1).astype(BF16)
        return top, bot

    def align_right(z, carry):
        for k in range(4):
            even, odd = (
                xr_buf[z, e, 4 * k : 4 * k + 4].reshape(4 * LINES, WIDTH) for e in range(2)
            )
            top, bot = straight(even, odd, left_half)
            both = [v.reshape(4, LINES, WIDTH) for v in (top, bot)]
            r_buf[z, 4 * TOK * k : 4 * TOK * (k + 1), :] = jnp.concatenate(both, 1).reshape(
                4 * TOK, WIDTH
            )
        return carry

    lax.fori_loop(0, DEPTHS, align_right, 0)

    def plane_of(role, own, t):
        up = t if own else -1 - t
        return lax.rem(depth + (up if role == 1 else -up) + DEPTHS, DEPTHS)

    def hand(part, role):
        return pltpu.make_async_remote_copy(
            src_ref=given_buf.at[part, role], dst_ref=taken.at[part, 1 - role],
            send_sem=e_send.at[part, role], recv_sem=e_recv.at[part, 1 - role],
            device_id=(row, above if role == 0 else below), device_id_type=MESH,
        )

    def multiply(part, carry):
        rows = pl.ds(part * PART, PART)
        arrived = xl_buf.at[:, :, :, rows]
        pltpu.make_async_copy(arrived, arrived, l_recv.at[part]).wait()
        owns = []
        for role in range(2):
            own = []
            for z in range(role * REACH, (role + 1) * REACH):
                even, odd = (xl_buf[z, e, :, rows, :].reshape(HALF * PART, WIDTH) for e in range(2))
                both = [v.reshape(HALF, PART, WIDTH) for v in straight(even, odd, left_half)]
                own.append(jnp.concatenate(both, 1).reshape(HALF * 2 * PART, WIDTH))
            owns.append(jnp.concatenate(own, 1))
        for own_columns in (False, True):
            for role in range(2):
                for t in range(0, REACH, 2):
                    starts = [
                        pl.multiple_of(plane_of(role, own_columns, t + k) * 2 * TOK, 2 * TOK)
                        for k in range(2)
                    ]
                    others = jnp.concatenate(
                        [
                            jnp.concatenate(
                                [r_buf[z, pl.ds(start, 2 * TOK), :] for start in starts], 0
                            )
                            for z in range(role * REACH, (role + 1) * REACH)
                        ],
                        1,
                    )
                    v = lax.dot_general(owns[role], others, NT, preferred_element_type=F32)
                    for k in range(2):
                        w = v[:, k * WIDTH : (k + 1) * WIDTH]
                        if own_columns:
                            kept[part, role, t + k] = w
                        else:
                            given_buf[part, role, t + k] = w.astype(BF16)
                if not own_columns:
                    hand(part, role).start()
        return carry

    lax.fori_loop(0, PARTS, multiply, 0)

    def give(part, carry):
        for role in range(2):
            hand(part, 1 - role).wait_recv()
        for t in range(REACH - 1, -1, -1):
            for role in range(2):
                w = kept[part, role, t] + taken[part, role, t].astype(F32)
                for r in range(HALF):
                    top = w[2 * PART * r : 2 * PART * r + PART]
                    bot = w[2 * PART * r + PART : 2 * PART * (r + 1)]
                    even = jnp.where(left_half, top, pltpu.roll(bot, TOK, 1))
                    odd = jnp.where(left_half, pltpu.roll(top, TOK, 1), bot)
                    p_buf[part, role, t, 0, r] = even.astype(BF16)
                    p_buf[part, role, t, 1, r] = odd.astype(BF16)
                plane = plane_of(role, True, t)
                dst = q_ref.at[channels[role], pl.ds(part * PART, PART)]
                for u in range(HALF):
                    r = lax.rem(slot + u, HALF)
                    for e in range(2):
                        src = p_buf.at[part, role, t, sides[e], r]

                        def remote(src=src, dst=dst, r=r, plane=plane, e=e):
                            pltpu.make_async_remote_copy(
                                src_ref=src, dst_ref=dst,
                                send_sem=p_send.at[part], recv_sem=p_recv.at[part],
                                device_id=(core * HALF + r, plane * 2 + sides[e]),
                                device_id_type=MESH,
                            ).start()

                        def local(src=src, dst=dst):
                            pltpu.make_async_copy(src, dst, p_recv.at[part]).start()

                        if t == 0 and u == 0 and e == 0:
                            pl.when(itself)(local)
                            pl.when(apart)(remote)
                        else:
                            remote()
        return carry

    lax.fori_loop(0, PARTS, give, 0)

    def put(part):
        rows = pl.ds(part * PART, PART)
        return pltpu.make_async_copy(out_buf.at[:, rows], out_ref.at[:, rows], out_sem.at[part])

    def finish(part, carry):
        come = q_ref.at[:, pl.ds(part * PART, PART)]
        pltpu.make_async_copy(come, come, p_recv.at[part]).wait()
        turned = jnp.swapaxes(q_ref[:, pl.ds(part * PART, PART), :], 0, 1)
        for u in range(PART):
            v = turned[u].astype(F32)
            v = v - jnp.mean(v, axis=0, keepdims=True)
            spread = jnp.mean(v * v, axis=0, keepdims=True)
            n = (v * lax.rsqrt(spread + EPS) * wide_buf[0] + wide_buf[1]).astype(BF16)
            o = lax.dot_general(n, ow_ref[...], TN, preferred_element_type=F32)
            line = part * PART + u
            out_buf[0, line] = (gate_buf[line] * o[:TOK]).astype(BF16)
            out_buf[1, line] = (gate_buf[LINES + line] * o[TOK:]).astype(BF16)
        put(part).start()
        return carry

    lax.fori_loop(0, PARTS, finish, 0)

    def drain(step, carry):
        forward(step)[1].wait_send()
        return carry

    lax.fori_loop(0, DEPTHS, drain, 0)

    for part in range(PARTS):
        for role in range(2):
            hand(part, role).wait_send()

    def finished(n):
        for buf, sem in ((sr_buf, r_send), (sl_buf, l_send)):
            sent = buf.at[pl.ds(0, n)]
            pltpu.make_async_copy(sent, sent, sem).wait()
        for part in range(PARTS):
            given = q_ref.at[pl.ds(0, n), pl.ds(part * PART, PART)]
            pltpu.make_async_copy(given, given, p_send.at[part]).wait()

    pl.when(itself)(functools.partial(finished, WIDTH - 2))
    pl.when(apart)(functools.partial(finished, WIDTH))
    for part in range(PARTS):
        put(part).wait()


def exchange(mask, pair, wl, wr, wg, gain, bias, og, ob, ow):
    whole = pl.BlockSpec(memory_space=pltpu.VMEM)
    return pl.pallas_call(
        exchange_kernel,
        out_shape=jax.ShapeDtypeStruct((2, LINES, TOK, WIDTH), BF16),
        in_specs=[pl.BlockSpec(memory_space=pltpu.SMEM)] + [whole] * 10,
        out_specs=pl.BlockSpec(memory_space=pl.ANY),
        scratch_shapes=[
            pltpu.VMEM((TOK, TOK, WIDTH), BF16),
            pltpu.VMEM((PART, WIDTH, WIDTH), BF16),
            pltpu.VMEM((PART, WIDTH, WIDTH), BF16),
            pltpu.VMEM((WIDTH, LINES, WIDTH), BF16),
            pltpu.VMEM((WIDTH, LINES, WIDTH), BF16),
            pltpu.VMEM((2 * REACH, 2, ROWS, LINES, WIDTH), BF16),
            pltpu.VMEM((2 * REACH, 2, HALF, LINES, WIDTH), BF16),
            pltpu.VMEM((DEPTHS, ROWS * TOK, WIDTH), BF16),
            pltpu.VMEM((PARTS, 2, REACH, 2, HALF, PART, WIDTH), BF16),
            pltpu.VMEM((WIDTH, LINES, WIDTH), BF16),
            pltpu.VMEM((TOK, TOK, WIDTH), F32),
            pltpu.VMEM((2, WIDTH, WIDTH), F32),
            pltpu.VMEM((2, LINES, TOK, WIDTH), BF16),
            pltpu.VMEM((PARTS, 2, REACH, HALF * 2 * PART, WIDTH), F32),
            pltpu.VMEM((PARTS, 2, REACH, HALF * 2 * PART, WIDTH), BF16),
            pltpu.VMEM((PARTS, 2, REACH, HALF * 2 * PART, WIDTH), BF16),
            pltpu.SemaphoreType.DMA((PARTS,)),
            pltpu.SemaphoreType.DMA,
            pltpu.SemaphoreType.DMA,
            pltpu.SemaphoreType.DMA((DEPTHS,)),
            pltpu.SemaphoreType.DMA((PARTS,)),
            pltpu.SemaphoreType.DMA((DEPTHS,)),
            pltpu.SemaphoreType.DMA((DEPTHS,)),
            pltpu.SemaphoreType.DMA((PARTS,)),
            pltpu.SemaphoreType.DMA((PARTS,)),
            pltpu.SemaphoreType.DMA((PARTS, 2)),
            pltpu.SemaphoreType.DMA((PARTS, 2)),
        ],
        compiler_params=pltpu.CompilerParams(
            collective_id=0, has_side_effects=True, vmem_limit_bytes=LIMIT
        ),
        name="exchange",
    )(mask, pair, wl, wr, wg, gain, bias, mask.reshape(DEPTHS, WIDTH), og, ob, ow)


def shards(
    pair_rep,
    token_mask,
    in_gain,
    in_bias,
    left_weight,
    right_weight,
    gate_weight,
    out_gain,
    out_bias,
    out_weight,
):
    flat = lambda v: v.reshape(1, WIDTH)
    out = exchange(
        token_mask,
        pair_rep,
        left_weight,
        right_weight,
        gate_weight,
        flat(in_gain),
        flat(in_bias),
        flat(out_gain),
        flat(out_bias),
        out_weight,
    )
    return out.reshape(TOK, TOK, WIDTH)


def solution(mesh):
    placed = (P("row", "col", None), P(), P(), P(), P(), P(), P(), P(), P(), P())
    return jax.shard_map(
        shards, mesh=mesh, in_specs=placed, out_specs=P("row", "col", None), check_vma=False
    )
```

time: 91.3 us -> 84.8 us (0.929)
  Pallas kernels: 91.1 us -> 82.4 us
  local copies, waits for them, and re-layouts: 0 us -> 2.26 us
    pallas_call x2 -> x1, Pallas kernels: 91.1 us -> 82.4 us  [exchange(): pl.pallas_call(exchange_kernel, out_shape=jax.ShapeDtypeStruct((2, LINES,...]
    unnamed x0 -> x1, local copies, waits for them, and re-layouts: none -> 2.26 us
where the time goes in v4:
time: 84.8 us; the launch traced here: 84.6 us
  Pallas kernels  82.4 us (97%)
  local copies, waits for them, and re-layouts  2.26 us (3%)
    pallas_call x1, Pallas kernels, exchange(): pl.pallas_call(exchange_kernel, out_shape=jax.ShapeDtypeStruct((2, LINES,...  82.4 us
    unnamed x1, local copies, waits for them, and re-layouts  2.26 us

profile of v4, /device:TPU:1, one launch (start us, length us, event | category | flops | bytes accessed | tf_op | source)
XLA Modules:
  0.0 84.6 jit_solution(3282642253711669262)
XLA Ops:
  0.0 82.4 %exchange.1 = bf16[2,32,64,128]{3,2,1,0:T(8,128)(2,1)} custom-call(s32[1024]{0:T(1024)} %mask_ref.1, bf16[64,64,128]{2,1,0:T(8,128)(2,1)} %x_ref.1, bf16[128,256]{1,0:T(8,128)(2,1)} %wl_ref.1, bf16[128,256]{1,0:T(8,128)(2,1)} %wr_ref.1, bf16[128,128]{1,0:T(8,128)(2,1)} %wg_ref.1, f32[1,128]{1,0:T(1,128)} %bitcast.8, f32[1,128]{1,0:T(1,128)} %bitcast.9, ...), custom_call_target="tpu_custom_call" | custom-call | tf_op jit(solution)/shard_map/exchange/pallas_call | solution.py:388
  82.4 2.3 %copy.12 = bf16[64,64,128]{2,1,0:T(8,128)(2,1)} copy(bf16[64,64,128]{2,1,0:T(8,128)(2,1)} %bitcast.6) | data formatting | bytes 2097152

commit v5 on v4

--- a/solution.py
+++ b/solution.py
@@ -35,9 +35,11 @@
 
 
 def exchange_kernel(
+    mask_hbm, x_hbm, wl_hbm, wr_hbm, wg_hbm, gain_hbm, bias_hbm, valid_hbm,
+    og_hbm, ob_hbm, ow_hbm,
+    out_ref,
     mask_ref, x_ref, wl_ref, wr_ref, wg_ref, gain_ref, bias_ref, valid_ref,
-    og_ref, ob_ref, ow_ref,
-    out_ref,
+    og_ref, ob_ref, ow_ref, in_sem,
     n_buf, tr_buf, tl_buf, sr_buf, sl_buf, xr_buf, xl_buf, r_buf, p_buf, q_ref, gate_buf, wide_buf, out_buf,
     kept, given_buf, taken,
     out_sem, r_send, l_send, r_recv, l_recv, f_send, f_recv, p_send, p_recv,
@@ -53,6 +55,27 @@
     itself = half == core
     apart = jnp.logical_not(itself)
 
+    loads = [
+        pltpu.make_async_copy(src, dst, in_sem.at[k])
+        for k, (src, dst) in enumerate(
+            (
+                (wl_hbm, wl_ref),
+                (wr_hbm, wr_ref),
+                (x_hbm, x_ref),
+                (gain_hbm, gain_ref),
+                (bias_hbm, bias_ref),
+                (valid_hbm, valid_ref),
+                (mask_hbm, mask_ref),
+                (wg_hbm, wg_ref),
+                (og_hbm, og_ref),
+                (ob_hbm, ob_ref),
+                (ow_hbm, ow_ref),
+            )
+        )
+    ]
+    for load in loads:
+        load.start()
+
     barrier = pltpu.get_barrier_semaphore()
 
     def hello(to_row, to_col):
@@ -74,6 +97,9 @@
         hello(row, above)
         hello(row, below)
 
+
+    for load in loads:
+        load.wait()
 
     gain, bias = gain_ref[...], bias_ref[...]
     wide = 2 * WIDTH
@@ -384,13 +410,17 @@
 
 
 def exchange(mask, pair, wl, wr, wg, gain, bias, og, ob, ow):
-    whole = pl.BlockSpec(memory_space=pltpu.VMEM)
+    hbm = pl.BlockSpec(memory_space=pl.ANY)
+    args = (mask, pair, wl, wr, wg, gain, bias, mask.reshape(DEPTHS, WIDTH), og, ob, ow)
     return pl.pallas_call(
         exchange_kernel,
         out_shape=jax.ShapeDtypeStruct((2, LINES, TOK, WIDTH), BF16),
-        in_specs=[pl.BlockSpec(memory_space=pltpu.SMEM)] + [whole] * 10,
+        in_specs=[hbm] * len(args),
         out_specs=pl.BlockSpec(memory_space=pl.ANY),
         scratch_shapes=[
+            pltpu.SMEM(mask.shape, mask.dtype),
+            *(pltpu.VMEM(v.shape, v.dtype) for v in args[1:]),
+            pltpu.SemaphoreType.DMA((len(args),)),
             pltpu.VMEM((TOK, TOK, WIDTH), BF16),
             pltpu.VMEM((PART, WIDTH, WIDTH), BF16),
             pltpu.VMEM((PART, WIDTH, WIDTH), BF16),
@@ -423,7 +453,7 @@
             collective_id=0, has_side_effects=True, vmem_limit_bytes=LIMIT
         ),
         name="exchange",
-    )(mask, pair, wl, wr, wg, gain, bias, mask.reshape(DEPTHS, WIDTH), og, ob, ow)
+    )(*args)
 
 
 def shards(

time: 84.8 us -> 83.5 us (0.985)
  Pallas kernels: 82.4 us -> 81.1 us
    pallas_call x1, Pallas kernels: 82.4 us -> 81.1 us  [exchange(): pl.pallas_call(exchange_kernel, out_shape=jax.ShapeDtypeStruct((2, LINES,...]
where the time goes in v5:
time: 83.5 us; the launch traced here: 83.4 us
  Pallas kernels  81.1 us (97%)
  local copies, waits for them, and re-layouts  2.26 us (3%)
    pallas_call x1, Pallas kernels, exchange(): pl.pallas_call(exchange_kernel, out_shape=jax.ShapeDtypeStruct((2, LINES,...  81.1 us
    unnamed x1, local copies, waits for them, and re-layouts  2.26 us

profile of v5, /device:TPU:1, one launch (start us, length us, event | category | flops | bytes accessed | tf_op | source)
XLA Modules:
  0.0 83.4 jit_solution(15416613238349252902)
XLA Ops:
  0.0 81.1 %exchange.1 = bf16[2,32,64,128]{3,2,1,0:T(8,128)(2,1)} custom-call(s32[1024]{0:T(1024)} %mask_hbm.1, bf16[64,64,128]{2,1,0:T(8,128)(2,1)} %x_hbm.1, bf16[128,256]{1,0:T(8,128)(2,1)} %wl_hbm.1, bf16[128,256]{1,0:T(8,128)(2,1)} %wr_hbm.1, bf16[128,128]{1,0:T(8,128)(2,1)} %wg_hbm.1, f32[1,128]{1,0:T(1,128)} %bitcast.8, f32[1,128]{1,0:T(1,128)} %bitcast.9, ...), custom_call_target="tpu_custom_call" | custom-call | tf_op jit(solution)/shard_map/exchange/pallas_call | solution.py:415
  81.1 2.3 %copy.12 = bf16[64,64,128]{2,1,0:T(8,128)(2,1)} copy(bf16[64,64,128]{2,1,0:T(8,128)(2,1)} %bitcast.6) | data formatting | bytes 2097152

commit v6 on v5

--- a/solution.py
+++ b/solution.py
@@ -181,7 +181,7 @@
             for d in range(CHIPS):
                 for e in range(2):
                     for role in range(2):
-                        send_to(role, REACH - 1 - u, d, e, False)
+                        send_to(role, 1 + u, d, e, False)
             return carry
 
         lax.fori_loop(0, REACH - 1, far, 0)

time: 83.5 us -> 84.4 us (1.011)
  Pallas kernels: 81.1 us -> 82 us
    pallas_call x1, Pallas kernels: 81.1 us -> 82 us  [exchange(): pl.pallas_call(exchange_kernel, out_shape=jax.ShapeDtypeStruct((2, LINES,...]
where the time goes in v6:
time: 84.4 us; the launch traced here: 84.3 us
  Pallas kernels  82 us (97%)
  local copies, waits for them, and re-layouts  2.26 us (3%)
    pallas_call x1, Pallas kernels, exchange(): pl.pallas_call(exchange_kernel, out_shape=jax.ShapeDtypeStruct((2, LINES,...  82 us
    unnamed x1, local copies, waits for them, and re-layouts  2.26 us

profile of v6, /device:TPU:1, one launch (start us, length us, event | category | flops | bytes accessed | tf_op | source)
XLA Modules:
  0.0 84.3 jit_solution(7785535211928401823)
XLA Ops:
  0.0 82.0 %exchange.1 = bf16[2,32,64,128]{3,2,1,0:T(8,128)(2,1)} custom-call(s32[1024]{0:T(1024)} %mask_hbm.1, bf16[64,64,128]{2,1,0:T(8,128)(2,1)} %x_hbm.1, bf16[128,256]{1,0:T(8,128)(2,1)} %wl_hbm.1, bf16[128,256]{1,0:T(8,128)(2,1)} %wr_hbm.1, bf16[128,128]{1,0:T(8,128)(2,1)} %wg_hbm.1, f32[1,128]{1,0:T(1,128)} %bitcast.8, f32[1,128]{1,0:T(1,128)} %bitcast.9, ...), custom_call_target="tpu_custom_call" | custom-call | tf_op jit(solution)/shard_map/exchange/pallas_call | solution.py:415
  82.0 2.3 %copy.12 = bf16[64,64,128]{2,1,0:T(8,128)(2,1)} copy(bf16[64,64,128]{2,1,0:T(8,128)(2,1)} %bitcast.6) | data formatting | bytes 2097152
